TPU v7x, 128 devices: a whole 4x4x4 slice. The times are simulated.
128 devices in a mesh: group: 32 (over z_lo, y, x), cls: 4 (over z_hi, core).
Axes of the slice: x: 4, y: 4, z: 4 (z_hi: 2, z_lo: 2; z = z_hi * 2 + z_lo), core: 2. Of those that a mesh axis runs over, the one named last changes fastest.
Arguments:
- features: bfloat16 [32768, 512], P(('group', 'cls')), may hold values from -6 to 6
- student_logits: bfloat16 [32768, 6656], P('group', 'cls'), may hold values from -100 to 320
- line_lengths: int32 [128], P(('group', 'cls')), may hold values from 64 to 256, as said below
- teacher_group: int32 [1], replicated, may hold values from 0 to 31
- pointwise_weight: bfloat16 [32, 512, 512], P('group'), may hold values from -0.25 to 0.25
- up_weight: bfloat16 [32, 512, 2048], P('group'), may hold values from -0.25 to 0.25
- down_weight: bfloat16 [32, 2048, 512], P('group'), may hold values from -0.125 to 0.125
- class_weight: bfloat16 [32, 512, 6656], P('group', None, 'cls'), may hold values from -9 to 9
- conv_kernel: bfloat16 [32, 3, 512], P('group'), may hold values from -3 to 3
- norm_gains: bfloat16 [32, 2, 512], P('group'), may hold values from 0.5 to 1.5
Outputs:
- divergence: float32 [32768], P(('group', 'cls'))
Inputs may be any that keep to these rules, and one draw needn't show every extreme that they name: `line_lengths`: every line has at least 64 frames in use, and some line uses all 256.
All inputs are finite; a program needn't handle non-finite values.
Results may differ from a plain program's by a relative error of at most 0.035.
Values may be sent and summed in bfloat16 or wider, within the bound.
A program may use at most 64 MiB of HBM per device.

v0:
```python
import math
import jax
import jax.numpy as jnp
from jax import lax
from jax.sharding import PartitionSpec as P

FRAMES = 256
EPS = 1e-06


def spread(x, axis, root):
    mine = lax.axis_index(axis) == root
    return lax.psum(jnp.where(mine, x, jnp.zeros_like(x)), axis)


def frame_mask(line_lengths):
    positions = jnp.arange(FRAMES, dtype=jnp.int32)
    return (positions[None, :] < line_lengths[:, None]).astype(jnp.float32).reshape(-1)


def rms_scale(values, gain):
    return (
        values
        * lax.rsqrt(jnp.mean(values * values, axis=-1, keepdims=True) + EPS)
        * gain.astype(jnp.float32)
    )


def teacher_layer(
    features, line_lengths, pointwise, up_proj, down_proj, kernel, gain_first, gain_second
):
    mask = frame_mask(line_lengths)
    inputs = features.astype(jnp.float32)
    masked = (inputs * mask[:, None]).reshape(-1, FRAMES, inputs.shape[1])
    padded = jnp.pad(masked, ((0, 0), (1, 1), (0, 0)))
    kern = kernel.astype(jnp.float32)
    conv = kern[0] * padded[:, :-2] + kern[1] * padded[:, 1:-1] + kern[2] * padded[:, 2:]
    conv = conv.reshape(inputs.shape).astype(jnp.bfloat16)
    resid = inputs + jnp.dot(conv, pointwise, preferred_element_type=jnp.float32)
    normed = rms_scale(resid, gain_first).astype(jnp.bfloat16)
    hidden = jax.nn.gelu(jnp.dot(normed, up_proj, preferred_element_type=jnp.float32)).astype(
        jnp.bfloat16
    )
    output = resid + jnp.dot(hidden, down_proj, preferred_element_type=jnp.float32)
    return (rms_scale(output, gain_second).astype(jnp.bfloat16), mask)


def row_kl(teacher_rows, student_rows):
    teach = teacher_rows.astype(jnp.float32)
    stud = student_rows.astype(jnp.float32)
    t_max = jnp.max(teach, axis=-1, keepdims=True)
    t_exp = jnp.exp(teach - t_max)
    t_sum = jnp.sum(t_exp, axis=-1)
    s_max = jnp.max(stud, axis=-1, keepdims=True)
    s_sum = jnp.sum(jnp.exp(stud - s_max), axis=-1)
    cross = jnp.sum(t_exp * (teach - stud), axis=-1)
    return cross / t_sum - (t_max[:, 0] + jnp.log(t_sum)) + (s_max[:, 0] + jnp.log(s_sum))


def blocked_rows(row_fn, teacher_logits, student_logits):
    rows = teacher_logits.shape[0]
    block = math.gcd(rows, 512)
    count = rows // block
    pairs = (teacher_logits.reshape(count, block, -1), student_logits.reshape(count, block, -1))
    result = lax.map(lambda pair: row_fn(pair[0], pair[1]), pairs)
    return result.reshape(rows)


def body(
    features,
    student_logits,
    line_lengths,
    teacher_group,
    pointwise_weight,
    up_weight,
    down_weight,
    class_weight,
    conv_kernel,
    norm_gains,
):
    source = teacher_group[0]
    small_params = jnp.concatenate([conv_kernel[0], norm_gains[0]], axis=0)
    pointwise, up_proj, down_proj, params_all, classes = (
        spread(pointwise_weight[0], "group", source),
        spread(up_weight[0], "group", source),
        spread(down_weight[0], "group", source),
        spread(small_params, "group", source),
        spread(class_weight[0], "group", source),
    )
    final, mask = teacher_layer(
        features,
        line_lengths,
        pointwise,
        up_proj,
        down_proj,
        params_all[:3],
        params_all[3],
        params_all[4],
    )
    teacher_logits = jnp.dot(
        lax.all_gather(final, "cls", axis=0, tiled=True),
        classes,
        preferred_element_type=jnp.float32,
    ).astype(jnp.bfloat16)
    teacher_rows, student_rows = (
        lax.all_to_all(teacher_logits, "cls", split_axis=0, concat_axis=1, tiled=True),
        lax.all_to_all(student_logits, "cls", split_axis=0, concat_axis=1, tiled=True),
    )
    divergence = blocked_rows(row_kl, teacher_rows, student_rows)
    return divergence * mask


def solution(mesh):
    return jax.shard_map(
        body,
        mesh=mesh,
        in_specs=(
            P(("group", "cls"), None),
            P("group", "cls"),
            P(("group", "cls")),
            P(),
            P("group", None, None),
            P("group", None, None),
            P("group", None, None),
            P("group", None, "cls"),
            P("group", None, None),
            P("group", None, None),
        ),
        out_specs=P(("group", "cls")),
        check_vma=False,
    )
```

profile of v0, /device:TPU:1, one launch (start us, length us, event | category | flops | bytes accessed | tf_op | source)
XLA Modules:
  0.0 452.9 jit_solution(15250304646624009235)
XLA Ops:
  7.2 1.5 select_bitcast_fusion
  8.7 0.9 copy-done
  9.5 1.5 select_bitcast_fusion.1
  11.0 0.7 copy-done.1
  11.8 1.3 select_bitcast_fusion.2
  13.1 0.8 select_bitcast_fusion.3
  13.9 0.0 all-reduce.4.cloned.1.call-update
  13.9 0.0 copy-start.3
  14.0 6.6 %all-to-all-start.1 = ((bf16[4,256,1664]{2,1,0:T(8,128)(2,1)}), bf16[4,256,1664]{2,1,0:T(8,128)(2,1)S(1)}, u32[]{:S(2)}, u32[]{:S(2)}) async-start(bf16[4,256,1664]{2,1,0:T(8,128)(2,1)} %bitcast.47), calls=%async_computation.1 | async-start | bytes 6815744 | tf_op jit(solution)/shard_map/all_to_all | solution.py:107
  21.3 72.6 %psum.35 = bf16[5,512]{1,0:T(8,128)(2,1)S(1)} all-reduce(bf16[5,512]{1,0:T(8,128)(2,1)S(1)} %maximum_select_fusion), channel_id=1, replica_groups=mesh['group'=32,'cls'=4] {'group'}, use_global_device_ids=true, to_apply=%region_0.1 | all-reduce | flops 2560 | bytes 10240 | tf_op jit(solution)/shard_map/psum | solution.py:13
  94.0 1.9 fusion.19
  95.9 237.7 %all-reduce.4.cloned.1.call-done = (bf16[512,512]{1,0:T(8,128)(2,1)}, bf16[2048,512]{1,0:T(8,128)(2,1)}, bf16[512,2048]{1,0:T(8,128)(2,1)}, bf16[512,1664]{1,0:T(8,128)(2,1)}) async-done(((bf16[512,512]{1,0:T(8,128)(2,1)}, bf16[2048,512]{1,0:T(8,128)(2,1)}, bf16[512,2048]{1,0:T(8,128)(2,1)}, bf16[512,1664]{1,0:T(8,128)(2,1)}), (bf16[512,512]{1,0:T(8,128)(2,1)}, bf16[2048,512]{1,0:T(8,128)(2,1)}, ...) | async-done | bytes 6422544 | tf_op jit(solution)/shard_map/psum | solution.py:13
  333.6 2.7 multiply_reduce_fusion.1
  336.3 4.9 %multiply_reduce_fusion = (f32[256]{0:T(256)S(1)}, f32[256,512]{1,0:T(8,128)}) fusion(f32[256,512]{1,0:T(8,128)} %get-tuple-element.30, bf16[2048,512]{1,0:T(8,128)(2,1)} %get-tuple-element.21, bf16[512,2048]{1,0:T(8,128)(2,1)} %get-tuple-element.22, f32[512]{0:T(512)S(1)} %bitcast.51, f32[256]{0:T(256)S(1)} %add_rsqrt_fusion.1), kind=kOutput, calls=%fused_computation.35 | convolution fusion | flops 1079246592 | bytes 5246976 | tf_op jit(solution)/shard_map/dot_general | solution.py:44
  341.2 1.9 multiply_convert_fusion
  343.0 0.0 all-gather.2.cloned.1.call-update
  343.0 43.1 %all-gather.2.cloned.1.call-done = bf16[1024,512]{1,0:T(8,128)(2,1)} async-done(((bf16[256,512]{1,0:T(8,128)(2,1)}), bf16[1024,512]{1,0:T(8,128)(2,1)}) %all-gather.2.cloned.1.call-update) | async-done | bytes 1048592 | tf_op jit(solution)/shard_map/all_gather | solution.py:101
  386.1 5.6 %convolution_convert_fusion = bf16[1024,1664]{1,0:T(8,128)(2,1)} fusion(bf16[1024,512]{1,0:T(8,128)(2,1)} %all-gather.2.cloned.1.call-done, bf16[512,1664]{1,0:T(8,128)(2,1)} %get-tuple-element.23), kind=kOutput, calls=%fused_computation.9 | convolution fusion | flops 1746534400 | bytes 6160384 | tf_op jit(solution)/shard_map/dot_general | solution.py:100
  391.7 5.0 %all-to-all-start = ((bf16[4,256,1664]{2,1,0:T(8,128)(2,1)}), bf16[4,256,1664]{2,1,0:T(8,128)(2,1)}, u32[]{:S(2)}, u32[]{:S(2)}) async-start(bf16[4,256,1664]{2,1,0:T(8,128)(2,1)} %bitcast.48), calls=%async_computation | async-start | bytes 6815744 | tf_op jit(solution)/shard_map/all_to_all | solution.py:106
  396.6 0.6 reduce_max.32
  397.2 39.8 %all-to-all-done = bf16[4,256,1664]{2,1,0:T(8,128)(2,1)} async-done(((bf16[4,256,1664]{2,1,0:T(8,128)(2,1)}), bf16[4,256,1664]{2,1,0:T(8,128)(2,1)}, u32[]{:S(2)}, u32[]{:S(2)}) %all-to-all-start) | async-done | bytes 3407904 | tf_op jit(solution)/shard_map/all_to_all | solution.py:106
  437.0 2.5 reduce_max.30
  439.5 6.0 %fusion.3 = (f32[256]{0:T(256)S(1)}, f32[256]{0:T(256)S(1)}, f32[256]{0:T(256)S(1)}) fusion(bf16[4,256,1664]{2,1,0:T(8,128)(2,1)} %all-to-all-done, bf16[4,256,1664]{2,1,0:T(8,128)(2,1)S(1)} %all-to-all-done.1, f32[256]{0:T(256)S(1)} %reduce_max.31, f32[256]{0:T(256)S(1)} %reduce_max.33), kind=kLoop, calls=%fused_computation.6 | loop fusion | flops 15334656 | bytes 6820864 | tf_op jit(solution)/shard_map/while/body/eval_jaxpr/reduce_sum | solution.py:56
  445.5 0.6 add_select_fusion
  (19 shorter events, 0.1 us)
Async XLA Ops:
  6.5 327.0 %all-reduce.4.cloned.1.call-start = ((), (), s32[]{:S(2)}) async-start(), calls=%async_computation.3 | async-start | bytes 12845056 | tf_op jit(solution)/shard_map/psum | solution.py:13
  7.2 2.3 copy-start
  9.5 2.2 copy-start.1
  11.8 1.3 copy-start.2
  13.9 7.3 %copy-start.3 = (bf16[1,3,512]{2,1,0:T(4,128)(2,1)S(1)}, bf16[1,3,512]{2,1,0:T(4,128)(2,1)}, u32[]{:S(2)}) copy-start(bf16[1,3,512]{2,1,0:T(4,128)(2,1)} %param.18) | copy-start | bytes 9220
  14.0 7.3 %copy-start.4 = (bf16[1,2,512]{2,1,0:T(2,128)(2,1)S(1)}, bf16[1,2,512]{2,1,0:T(2,128)(2,1)}, u32[]{:S(2)}) copy-start(bf16[1,2,512]{2,1,0:T(2,128)(2,1)} %param.19) | copy-start | bytes 6148
  14.0 377.7 %all-to-all-start.1 = ((bf16[4,256,1664]{2,1,0:T(8,128)(2,1)}), bf16[4,256,1664]{2,1,0:T(8,128)(2,1)S(1)}, u32[]{:S(2)}, u32[]{:S(2)}) async-start(bf16[4,256,1664]{2,1,0:T(8,128)(2,1)} %bitcast.47), calls=%async_computation.1 | async-start | bytes 6815744 | tf_op jit(solution)/shard_map/all_to_all | solution.py:107
  20.6 365.5 %all-gather.2.cloned.1.call-start = ((), (), s32[]{:S(2)}) async-start(), calls=%async_computation.2 | async-start | bytes 1310720 | tf_op jit(solution)/shard_map/all_gather | solution.py:101
  391.7 45.3 %all-to-all-start = ((bf16[4,256,1664]{2,1,0:T(8,128)(2,1)}), bf16[4,256,1664]{2,1,0:T(8,128)(2,1)}, u32[]{:S(2)}, u32[]{:S(2)}) async-start(bf16[4,256,1664]{2,1,0:T(8,128)(2,1)} %bitcast.48), calls=%async_computation | async-start | bytes 6815744 | tf_op jit(solution)/shard_map/all_to_all | solution.py:106
Sparse Core Ops, SparseCore 0:
  14.1 319.4 all-reduce.3
  343.2 42.8 all-gather.1
where the time goes:
time: 454 us; the launch traced here: 453 us
  waiting for transfers between devices  321 us (71%)
  blocking collectives  72.6 us (16%)
  other arithmetic  18.6 us (4%)
  between operations  14.8 us (3%)
  matrix products  13.2 us (3%)
  starting transfers between devices  11.6 us (3%)
    psum x1, waiting for transfers between devices, spread(): return lax.psum(jnp.where(mine, x, jnp.zeros_like(x)), axis)  238 us
    psum x1, blocking collectives, spread(): return lax.psum(jnp.where(mine, x, jnp.zeros_like(x)), axis)  72.6 us
    all_gather x1, waiting for transfers between devices, body(): lax.all_gather(final, 'cls', axis=0, tiled=True)  43.1 us
    all_to_all x1, waiting for transfers between devices, body(): lax.all_to_all(teacher_logits, 'cls', split_axis=0, concat_axis=1, tiled=...  39.8 us
  transfers between devices with their start and end apart: 4, of which 3 were waited for; matrix products, arithmetic and copies ran while one was open for 4% of the time, Pallas kernels for 0%

commit v1 on v0

--- a/solution.py
+++ b/solution.py
@@ -98,7 +98,9 @@
         params_all[4],
     )
     teacher_logits = jnp.dot(
-        lax.all_gather(final, "cls", axis=0, tiled=True),
+        jnp.concatenate(
+            lax.all_to_all(jnp.stack([final] * lax.axis_size("cls")), "cls", 0, 0), axis=0
+        ),
         classes,
         preferred_element_type=jnp.float32,
     ).astype(jnp.bfloat16)

time: 454 us -> 486 us (1.070)
  blocking collectives: 72.6 us -> 113 us
    all_gather x1 -> x0, waiting for transfers between devices: 43.1 us -> none  [body(): lax.all_gather(final, 'cls', axis=0, tiled=True)]
    all_to_all x0 -> x1, blocking collectives: none -> 40.2 us  [body(): lax.all_to_all(jnp.stack([final] * lax.axis_size('cls')), 'cls', 0, 0)]
    all_to_all x1, waiting for transfers between devices: 0.01 us -> 34.7 us  [body(): lax.all_to_all(student_logits, 'cls', split_axis=0, concat_axis=1, tiled=...]
    psum x1, waiting for transfers between devices: 238 us -> 245 us  [spread(): return lax.psum(jnp.where(mine, x, jnp.zeros_like(x)), axis)]
  transfers between devices with their start and end apart: 4 -> 3, of which waited for: 3 -> 3; matrix products, arithmetic and copies ran while one was open for 4% -> 1% of each run, Pallas kernels for 0% -> 0%
where the time goes in v1:
time: 486 us
  waiting for transfers between devices  320 us (66%)
  blocking collectives  113 us (23%)
  other arithmetic  15.1 us (3%)
  between operations  14.9 us (3%)
  matrix products  10.5 us (2%)
  starting transfers between devices  10.4 us (2%)
    psum x1, waiting for transfers between devices, spread(): return lax.psum(jnp.where(mine, x, jnp.zeros_like(x)), axis)  245 us
    psum x1, blocking collectives, spread(): return lax.psum(jnp.where(mine, x, jnp.zeros_like(x)), axis)  72.9 us
    all_to_all x1, blocking collectives, body(): lax.all_to_all(jnp.stack([final] * lax.axis_size('cls')), 'cls', 0, 0)  40.2 us
    all_to_all x1, waiting for transfers between devices, body(): lax.all_to_all(teacher_logits, 'cls', split_axis=0, concat_axis=1, tiled=...  39.8 us
    all_to_all x1, waiting for transfers between devices, body(): lax.all_to_all(student_logits, 'cls', split_axis=0, concat_axis=1, tiled=...  34.7 us
  transfers between devices with their start and end apart: 3, of which 3 were waited for; matrix products, arithmetic and copies ran while one was open for 1% of the time, Pallas kernels for 0%

profile of v1, /device:TPU:1, one launch (start us, length us, event | category | flops | bytes accessed | tf_op | source)
XLA Modules:
  0.0 485.6 jit_solution(11557771372432222627)
XLA Ops:
  7.2 1.5 select_bitcast_fusion
  8.7 0.9 copy-done
  9.5 1.5 select_bitcast_fusion.1
  11.0 0.7 copy-done.1
  11.8 1.3 select_bitcast_fusion.2
  13.1 0.8 select_bitcast_fusion.3
  14.7 72.9 %psum.35 = bf16[5,512]{1,0:T(8,128)(2,1)S(1)} all-reduce(bf16[5,512]{1,0:T(8,128)(2,1)S(1)} %maximum_select_fusion), channel_id=1, replica_groups=mesh['group'=32,'cls'=4] {'group'}, use_global_device_ids=true, to_apply=%region_0.1 | all-reduce | flops 2560 | bytes 10240 | tf_op jit(solution)/shard_map/psum | solution.py:13
  87.7 0.1 fusion.19
  87.8 245.4 %all-reduce.4.cloned.1.call-done = (bf16[512,512]{1,0:T(8,128)(2,1)}, bf16[2048,512]{1,0:T(8,128)(2,1)}, bf16[512,2048]{1,0:T(8,128)(2,1)}, bf16[512,1664]{1,0:T(8,128)(2,1)}) async-done(((bf16[512,512]{1,0:T(8,128)(2,1)}, bf16[2048,512]{1,0:T(8,128)(2,1)}, bf16[512,2048]{1,0:T(8,128)(2,1)}, bf16[512,1664]{1,0:T(8,128)(2,1)}), (bf16[512,512]{1,0:T(8,128)(2,1)}, bf16[2048,512]{1,0:T(8,128)(2,1)}, ...) | async-done | bytes 6422544 | tf_op jit(solution)/shard_map/psum | solution.py:13
  333.2 1.7 multiply_reduce_fusion.1
  334.9 0.1 copy-done.6
  334.9 3.3 multiply_reduce_fusion
  338.2 0.1 multiply_convert_fusion
  338.3 0.1 stack.2
  338.4 40.2 %all_to_all.31 = bf16[4,256,512]{2,1,0:T(8,128)(2,1)} all-to-all(bf16[4,256,512]{2,1,0:T(8,128)(2,1)S(1)} %stack.2), channel_id=1, replica_groups=mesh['group'=32,'cls'=4] {'cls'}, dimensions={0} | all-to-all | bytes 2097152 | tf_op jit(solution)/shard_map/all_to_all | solution.py:102
  378.6 4.7 all-to-all-start.2
  383.4 5.6 %convolution_convert_fusion = bf16[1024,1664]{1,0:T(8,128)(2,1)} fusion(bf16[1024,512]{1,0:T(8,128)(2,1)} %bitcast.50, bf16[512,1664]{1,0:T(8,128)(2,1)} %get-tuple-element.23), kind=kOutput, calls=%fused_computation.9 | convolution fusion | flops 1746534400 | bytes 6160384 | tf_op jit(solution)/shard_map/dot_general | solution.py:100
  388.9 34.7 %all-to-all-done.2 = bf16[4,256,1664]{2,1,0:T(8,128)(2,1)S(1)} async-done(((bf16[4,256,1664]{2,1,0:T(8,128)(2,1)}), bf16[4,256,1664]{2,1,0:T(8,128)(2,1)S(1)}, u32[]{:S(2)}, u32[]{:S(2)}) %all-to-all-start.2) | async-done | bytes 3407904 | tf_op jit(solution)/shard_map/all_to_all | solution.py:109
  423.6 5.6 %all-to-all-start.1 = ((bf16[4,256,1664]{2,1,0:T(8,128)(2,1)}), bf16[4,256,1664]{2,1,0:T(8,128)(2,1)}, u32[]{:S(2)}, u32[]{:S(2)}) async-start(bf16[4,256,1664]{2,1,0:T(8,128)(2,1)} %bitcast.49), calls=%async_computation.1 | async-start | bytes 6815744 | tf_op jit(solution)/shard_map/all_to_all | solution.py:108
  429.2 0.6 reduce_max.32
  429.8 39.8 %all-to-all-done.1 = bf16[4,256,1664]{2,1,0:T(8,128)(2,1)} async-done(((bf16[4,256,1664]{2,1,0:T(8,128)(2,1)}), bf16[4,256,1664]{2,1,0:T(8,128)(2,1)}, u32[]{:S(2)}, u32[]{:S(2)}) %all-to-all-start.1) | async-done | bytes 3407904 | tf_op jit(solution)/shard_map/all_to_all | solution.py:108
  469.6 2.5 reduce_max.30
  472.1 6.0 %fusion.3 = (f32[256]{0:T(256)S(1)}, f32[256]{0:T(256)S(1)}, f32[256]{0:T(256)S(1)}) fusion(bf16[4,256,1664]{2,1,0:T(8,128)(2,1)} %all-to-all-done.1, bf16[4,256,1664]{2,1,0:T(8,128)(2,1)S(1)} %all-to-all-done.2, f32[256]{0:T(256)S(1)} %reduce_max.31, f32[256]{0:T(256)S(1)} %reduce_max.33), kind=kLoop, calls=%fused_computation.6 | loop fusion | flops 15334656 | bytes 6820864 | tf_op jit(solution)/shard_map/while/body/eval_jaxpr/reduce_sum | solution.py:56
  478.1 0.6 add_select_fusion
  (22 shorter events, 0.1 us)
Async XLA Ops:
  6.5 326.6 %all-reduce.4.cloned.1.call-start = ((), (), s32[]{:S(2)}) async-start(), calls=%async_computation.3 | async-start | bytes 12845056 | tf_op jit(solution)/shard_map/psum | solution.py:13
  7.2 2.3 copy-start
  9.5 2.2 copy-start.1
  11.8 1.3 copy-start.2
  13.9 0.7 copy-start.4
  13.9 0.7 copy-start.5
  13.9 73.7 %copy-start.3 = (bf16[256,512]{1,0:T(8,128)(2,1)S(1)}, bf16[256,512]{1,0:T(8,128)(2,1)}, u32[]{:S(2)}) copy-start(bf16[256,512]{1,0:T(8,128)(2,1)} %param.10) | copy-start | bytes 786436
  333.2 1.7 copy-start.6
  378.6 45.0 %all-to-all-start.2 = ((bf16[4,256,1664]{2,1,0:T(8,128)(2,1)}), bf16[4,256,1664]{2,1,0:T(8,128)(2,1)S(1)}, u32[]{:S(2)}, u32[]{:S(2)}) async-start(bf16[4,256,1664]{2,1,0:T(8,128)(2,1)} %bitcast.48), calls=%async_computation.2 | async-start | bytes 6815744 | tf_op jit(solution)/shard_map/all_to_all | solution.py:109
  423.6 46.0 %all-to-all-start.1 = ((bf16[4,256,1664]{2,1,0:T(8,128)(2,1)}), bf16[4,256,1664]{2,1,0:T(8,128)(2,1)}, u32[]{:S(2)}, u32[]{:S(2)}) async-start(bf16[4,256,1664]{2,1,0:T(8,128)(2,1)} %bitcast.49), calls=%async_computation.1 | async-start | bytes 6815744 | tf_op jit(solution)/shard_map/all_to_all | solution.py:108
Sparse Core Ops, SparseCore 0:
  14.1 319.0 all-reduce.3
